TPU v7x, 32 devices: a whole 2x2x4 slice. The times are simulated.
32 devices in a mesh: fsdp: 4 (over y, x), ctx: 2 (over core), tp: 4 (over z).
Axes of the slice: x: 2, y: 2, z: 4, core: 2. Of those that a mesh axis runs over, the one named last changes fastest.
Arguments:
- block_input: float32 [4, 1024, 2048], P('fsdp', 'ctx'), may hold values from -6 to 6
- cotangent: float32 [4, 1024, 2048], P('fsdp', 'ctx'), may hold values from -6 to 6
- w_query: bfloat16 [2048, 2048], P(('fsdp', 'ctx'), 'tp'), may hold values from -0.125 to 0.125
- w_key: bfloat16 [2048, 512], P(('fsdp', 'ctx'), 'tp'), may hold values from -0.125 to 0.125
- w_value: bfloat16 [2048, 512], P(('fsdp', 'ctx'), 'tp'), may hold values from -0.125 to 0.125
- w_output: bfloat16 [2048, 2048], P('tp', ('fsdp', 'ctx')), may hold values from -4 to 4
- w_gate: bfloat16 [2048, 8192], P(('fsdp', 'ctx'), 'tp'), may hold values from -0.125 to 0.125
- w_up: bfloat16 [2048, 8192], P(('fsdp', 'ctx'), 'tp'), may hold values from -0.125 to 0.125
- w_down: bfloat16 [8192, 2048], P('tp', ('fsdp', 'ctx')), may hold values from -0.0625 to 0.0625
- attn_gain: bfloat16 [2048], P(('fsdp', 'ctx')), may hold values from 0.5 to 1.5
- ffn_gain: bfloat16 [2048], P(('fsdp', 'ctx')), may hold values from 0.5 to 1.5
Outputs:
- block_output: float32 [4, 1024, 2048], P('fsdp', 'ctx')
- input_grad: float32 [4, 1024, 2048], P('fsdp', 'ctx')
- grad_query: float32 [2048, 2048], P(('fsdp', 'ctx'), 'tp')
- grad_key: float32 [2048, 512], P(('fsdp', 'ctx'), 'tp')
- grad_value: float32 [2048, 512], P(('fsdp', 'ctx'), 'tp')
- grad_output: float32 [2048, 2048], P('tp', ('fsdp', 'ctx'))
- grad_gate: float32 [2048, 8192], P(('fsdp', 'ctx'), 'tp')
- grad_up: float32 [2048, 8192], P(('fsdp', 'ctx'), 'tp')
- grad_down: float32 [8192, 2048], P('tp', ('fsdp', 'ctx'))
- grad_attn_gain: float32 [2048], P(('fsdp', 'ctx'))
- grad_ffn_gain: float32 [2048], P(('fsdp', 'ctx'))
All inputs are finite; a program needn't handle non-finite values.
Results may differ from a plain program's by a relative error of at most 0.013.
Values may be sent and summed in bfloat16 or wider, within the bound.
No kernel may reach another device: no remote copies, remote signals or barrier semaphores. Data moves between devices by JAX's collectives and lax.ppermute only.
A program may use at most 256 MiB of HBM per device.

v0:
```python
import jax
import jax.numpy as jnp
from jax import lax
from jax.sharding import PartitionSpec as P

HD = 64
EPS = 1e-05
BASE = 500000.0
NEG = -1e30


def shifted(shard, axis, by):
    count = lax.axis_size(axis)
    pairs = [(i, i + by) for i in range(count) if 0 <= i + by < count]
    return lax.ppermute(shard, axis, pairs)


def rotate(values, positions, sign):
    half = values.shape[-1] // 2
    inverse = BASE ** (-(jnp.arange(half, dtype=jnp.float32) * 2.0) / values.shape[-1])
    angle = positions.astype(jnp.float32)[:, None] * inverse[None, :]
    cosine = jnp.cos(angle)[:, None, :]
    sine = sign * jnp.sin(angle)[:, None, :]
    first = values[..., :half]
    second = values[..., half:]
    return jnp.concatenate(
        [first * cosine - second * sine, second * cosine + first * sine], axis=-1
    )


def norm_forward(rows, gain):
    scale = lax.rsqrt(jnp.mean(rows * rows, axis=-1, keepdims=True) + EPS)
    return (rows * scale * gain, scale)


def norm_backward(rows, scale, gain, grad):
    weighted = grad * gain
    d_rows = scale * weighted - rows * scale**3 * jnp.mean(weighted * rows, axis=-1, keepdims=True)
    return (d_rows, jnp.sum(grad * rows * scale, axis=0))


def forward_block(queries, keys, vals, allow, scale):
    scores = jnp.einsum("gbd,kd->gbk", queries, keys, preferred_element_type=jnp.float32) * scale
    scores = jnp.where(allow[None], scores, NEG)
    top = jnp.max(scores, axis=-1, keepdims=True)
    total = top[..., 0] + jnp.log(jnp.sum(jnp.exp(scores - top), axis=-1))
    probs = jnp.exp(scores - total[..., None]).astype(jnp.bfloat16)
    out = jnp.einsum("gbk,kd->gbd", probs, vals, preferred_element_type=jnp.float32)
    return (out.astype(jnp.bfloat16), total)


def backward_block(queries, keys, vals, allow, total, grad_out, out, scale):
    scores = jnp.einsum("gbd,kd->gbk", queries, keys, preferred_element_type=jnp.float32) * scale
    scores = jnp.where(allow[None], scores, NEG)
    probs = jnp.exp(scores - total[..., None])
    rounded = probs.astype(jnp.bfloat16)
    d_vals = jnp.einsum("gbk,gbd->kd", rounded, grad_out, preferred_element_type=jnp.float32)
    d_probs = jnp.einsum("gbd,kd->gbk", grad_out, vals, preferred_element_type=jnp.float32)
    delta = jnp.sum(grad_out.astype(jnp.float32) * out.astype(jnp.float32), axis=-1)
    d_scores = (probs * (d_probs - delta[..., None]) * scale).astype(jnp.bfloat16)
    d_query = jnp.einsum("gbk,kd->gbd", d_scores, keys, preferred_element_type=jnp.float32)
    d_keys = jnp.einsum("gbk,gbd->kd", d_scores, queries, preferred_element_type=jnp.float32)
    return (d_query, d_keys, d_vals)


def split_blocks(tensor, count, block):
    return tensor.reshape((tensor.shape[0], count, block) + tensor.shape[2:]).swapaxes(0, 1)


def attention_forward(grouped, keys, vals, allow, block, scale):

    def per_head(items):
        head_q, head_k, head_v = items
        groups, rows, width = head_q.shape
        count = rows // block
        outs, totals = lax.map(
            lambda piece: forward_block(piece[0], head_k, head_v, piece[1], scale),
            (split_blocks(head_q, count, block), allow.reshape(count, block, allow.shape[1])),
        )
        return (
            outs.swapaxes(0, 1).reshape(groups, rows, width),
            totals.swapaxes(0, 1).reshape(groups, rows),
        )

    return lax.map(per_head, (grouped, keys, vals))


def attention_backward(grouped, keys, vals, allow, totals, grads, outs, block, scale):

    def per_head(items):
        head_q, head_k, head_v, head_t, head_g, head_o = items
        groups, rows, width = head_q.shape
        count = rows // block

        def step(carry, piece):
            d_query, d_keys, d_vals = backward_block(
                piece[0], head_k, head_v, piece[1], piece[2], piece[3], piece[4], scale
            )
            return ((carry[0] + d_keys, carry[1] + d_vals), d_query)

        zeros = jnp.zeros(head_k.shape, jnp.float32)
        pieces = (
            split_blocks(head_q, count, block),
            allow.reshape(count, block, allow.shape[1]),
            split_blocks(head_t, count, block),
            split_blocks(head_g, count, block),
            split_blocks(head_o, count, block),
        )
        (d_keys, d_vals), d_query = lax.scan(step, (zeros, zeros), pieces)
        return (d_query.swapaxes(0, 1).reshape(groups, rows, width), d_keys, d_vals)

    return lax.map(per_head, (grouped, keys, vals, totals, grads, outs))


def dotf(left, right):
    return jnp.dot(left, right, preferred_element_type=jnp.float32)


def body(
    block_input,
    cotangent,
    w_query,
    w_key,
    w_value,
    w_output,
    w_gate,
    w_up,
    w_down,
    attn_gain,
    ffn_gain,
):
    wq, wk, wv, wo, wg, wu, wd, gain_qa, gain_qf = (
        lax.all_gather(w_query, ("fsdp", "ctx"), axis=0, tiled=True),
        lax.all_gather(w_key, ("fsdp", "ctx"), axis=0, tiled=True),
        lax.all_gather(w_value, ("fsdp", "ctx"), axis=0, tiled=True),
        lax.all_gather(w_output, ("fsdp", "ctx"), axis=1, tiled=True),
        lax.all_gather(w_gate, ("fsdp", "ctx"), axis=0, tiled=True),
        lax.all_gather(w_up, ("fsdp", "ctx"), axis=0, tiled=True),
        lax.all_gather(w_down, ("fsdp", "ctx"), axis=1, tiled=True),
        lax.all_gather(attn_gain, ("fsdp", "ctx"), axis=0, tiled=True),
        lax.all_gather(ffn_gain, ("fsdp", "ctx"), axis=0, tiled=True),
    )
    rows = block_input[0]
    cot = cotangent[0]
    local = rows.shape[0]
    block = min(512, local)
    scale = HD ** (-0.5)
    heads = wq.shape[1] // HD
    kv_heads = wk.shape[1] // HD
    groups = heads // kv_heads
    place = lax.axis_index("ctx")
    positions = place * local + jnp.arange(local, dtype=jnp.int32)
    gain_a = gain_qa.astype(jnp.float32)
    gain_f = gain_qf.astype(jnp.float32)
    normed_f, scale_a = norm_forward(rows, gain_a)
    normed = normed_f.astype(jnp.bfloat16)
    query = dotf(normed, wq).reshape(local, heads, HD)
    keys = dotf(normed, wk).reshape(local, kv_heads, HD)
    vals = dotf(normed, wv)
    query_rot = rotate(query, positions, 1.0).astype(jnp.bfloat16)
    keys_rot = rotate(keys, positions, 1.0).astype(jnp.bfloat16).reshape(local, kv_heads * HD)
    vals_b = vals.astype(jnp.bfloat16)
    keys_prev, vals_prev = shifted((keys_rot, vals_b), "ctx", 1)
    all_keys = (
        jnp.concatenate([keys_prev, keys_rot], axis=0)
        .reshape(2 * local, kv_heads, HD)
        .transpose(1, 0, 2)
    )
    all_vals = (
        jnp.concatenate([vals_prev, vals_b], axis=0)
        .reshape(2 * local, kv_heads, HD)
        .transpose(1, 0, 2)
    )
    grouped = query_rot.reshape(local, kv_heads, groups, HD).transpose(1, 2, 0, 3)
    index = jnp.arange(local, dtype=jnp.int32)
    earlier = jnp.broadcast_to(place > 0, (local, local))
    causal = index[None, :] <= index[:, None]
    allow = jnp.concatenate([earlier, causal], axis=1)
    attn, totals = attention_forward(grouped, all_keys, all_vals, allow, block, scale)
    attn_flat = attn.transpose(2, 0, 1, 3).reshape(local, heads * HD)
    hidden = rows + lax.psum(dotf(attn_flat, wo), "tp")
    hnorm_f, scale_f = norm_forward(hidden, gain_f)
    hnorm = hnorm_f.astype(jnp.bfloat16)
    gate = dotf(hnorm, wg)
    up = dotf(hnorm, wu)
    sigma = jax.nn.sigmoid(gate)
    active = gate * sigma
    inner = (active * up).astype(jnp.bfloat16)
    out = hidden + lax.psum(dotf(inner, wd).astype(jnp.bfloat16), "tp").astype(jnp.float32)
    cot_b = cot.astype(jnp.bfloat16)
    d_inner = dotf(cot_b, wd.T)
    d_gate = (d_inner * up * sigma * (1.0 + gate * (1.0 - sigma))).astype(jnp.bfloat16)
    d_up = (d_inner * active).astype(jnp.bfloat16)
    d_hnorm = lax.psum(dotf(d_gate, wg.T) + dotf(d_up, wu.T), "tp")
    d_norm, g_ffn = norm_backward(hidden, scale_f, gain_f, d_hnorm)
    d_hidden = cot + d_norm
    dh_b = d_hidden.astype(jnp.bfloat16)
    d_attn = (
        dotf(dh_b, wo.T)
        .astype(jnp.bfloat16)
        .reshape(local, kv_heads, groups, HD)
        .transpose(1, 2, 0, 3)
    )
    d_query, d_keys, d_vals = attention_backward(
        grouped, all_keys, all_vals, allow, totals, d_attn, attn, block, scale
    )
    keys_grad = d_keys.transpose(1, 0, 2).reshape(2 * local, kv_heads * HD)
    vals_grad = d_vals.transpose(1, 0, 2).reshape(2 * local, kv_heads * HD)
    keys_back, vals_back = shifted((keys_grad[:local], vals_grad[:local]), "ctx", -1)
    keys_own = keys_grad[local:] + keys_back
    vals_own = vals_grad[local:] + vals_back
    d_query = d_query.transpose(2, 0, 1, 3).reshape(local, heads, HD)
    dq_b = rotate(d_query, positions, -1.0).astype(jnp.bfloat16).reshape(local, heads * HD)
    dk_b = (
        rotate(keys_own.reshape(local, kv_heads, HD), positions, -1.0)
        .astype(jnp.bfloat16)
        .reshape(local, kv_heads * HD)
    )
    dv_b = vals_own.astype(jnp.bfloat16)
    d_normed = lax.psum(dotf(dq_b, wq.T) + dotf(dk_b, wk.T) + dotf(dv_b, wv.T), "tp")
    d_rows, g_attn = norm_backward(rows, scale_a, gain_a, d_normed)
    d_input = d_hidden + d_rows
    s_query, s_key, s_value, s_output, s_gate, s_up, s_down, s_attn, s_ffn = (
        lax.psum_scatter(dotf(normed.T, dq_b), ("fsdp", "ctx"), scatter_dimension=0, tiled=True),
        lax.psum_scatter(dotf(normed.T, dk_b), ("fsdp", "ctx"), scatter_dimension=0, tiled=True),
        lax.psum_scatter(dotf(normed.T, dv_b), ("fsdp", "ctx"), scatter_dimension=0, tiled=True),
        lax.psum_scatter(dotf(attn_flat.T, dh_b), ("fsdp", "ctx"), scatter_dimension=1, tiled=True),
        lax.psum_scatter(dotf(hnorm.T, d_gate), ("fsdp", "ctx"), scatter_dimension=0, tiled=True),
        lax.psum_scatter(dotf(hnorm.T, d_up), ("fsdp", "ctx"), scatter_dimension=0, tiled=True),
        lax.psum_scatter(dotf(inner.T, cot_b), ("fsdp", "ctx"), scatter_dimension=1, tiled=True),
        lax.psum_scatter(g_attn, ("fsdp", "ctx"), scatter_dimension=0, tiled=True),
        lax.psum_scatter(g_ffn, ("fsdp", "ctx"), scatter_dimension=0, tiled=True),
    )
    return (
        out[None],
        d_input[None],
        s_query,
        s_key,
        s_value,
        s_output,
        s_gate,
        s_up,
        s_down,
        s_attn,
        s_ffn,
    )


def solution(mesh):
    placed = (
        P("fsdp", "ctx", None),
        P("fsdp", "ctx", None),
        P(("fsdp", "ctx"), "tp"),
        P(("fsdp", "ctx"), "tp"),
        P(("fsdp", "ctx"), "tp"),
        P("tp", ("fsdp", "ctx")),
        P(("fsdp", "ctx"), "tp"),
        P(("fsdp", "ctx"), "tp"),
        P("tp", ("fsdp", "ctx")),
        P(("fsdp", "ctx")),
        P(("fsdp", "ctx")),
    )
    return jax.shard_map(
        body,
        mesh=mesh,
        in_specs=placed,
        out_specs=(
            P("fsdp", "ctx", None),
            P("fsdp", "ctx", None),
            P(("fsdp", "ctx"), "tp"),
            P(("fsdp", "ctx"), "tp"),
            P(("fsdp", "ctx"), "tp"),
            P("tp", ("fsdp", "ctx")),
            P(("fsdp", "ctx"), "tp"),
            P(("fsdp", "ctx"), "tp"),
            P("tp", ("fsdp", "ctx")),
            P(("fsdp", "ctx")),
            P(("fsdp", "ctx")),
        ),
        check_vma=False,
    )
```

profile of v0, /device:TPU:0, one launch (start us, length us, event | category | flops | bytes accessed | tf_op | source)
XLA Modules:
  0.0 1437.5 jit_solution(5688634115593749319)
XLA Ops:
  8.6 10.4 all-gather
  19.0 10.7 all_gather.29
  30.0 3.0 fusion.52
  36.5 2.9 collective-permute-start
  39.4 8.9 all_gather.30
  51.5 2.9 collective-permute-start.1
  59.2 3.9 copy.28
  63.2 2.9 fusion.65
  66.3 12.7 while.10
  79.0 4.0 all-gather.10.cloned.1.call-done
  83.0 4.9 fusion.86
  89.7 9.1 all-gather.1
  98.8 144.2 %all-reduce.9.cloned.1.call-done = f32[512,2048]{1,0:T(8,128)} async-done(((f32[512,2048]{1,0:T(8,128)}), f32[512,2048]{1,0:T(8,128)}) %all-reduce.9.cloned.1.call-update) | async-done | bytes 4194320 | tf_op jit(solution)/shard_map/psum | solution.py:181
  243.0 4.0 multiply_reduce_fusion.2
  250.8 47.2 %all-gather.12.cloned.1.call-done = bf16[2048,2048]{1,0:T(8,128)(2,1)} async-done(((bf16[256,2048]{1,0:T(8,128)(2,1)}), bf16[2048,2048]{1,0:T(8,128)(2,1)}) %all-gather.12.cloned.1.call-update) | async-done | bytes 8388624 | tf_op jit(solution)/shard_map/all_gather | solution.py:137
  298.0 10.5 fusion.87
  308.6 45.5 %all-gather.14.cloned.1.call-done = bf16[2048,2048]{1,0:T(8,128)(2,1)} async-done(((bf16[256,2048]{1,0:T(8,128)(2,1)}), bf16[2048,2048]{1,0:T(8,128)(2,1)}) %all-gather.14.cloned.1.call-update) | async-done | bytes 8388624 | tf_op jit(solution)/shard_map/all_gather | solution.py:138
  354.1 10.5 fusion.88
  364.6 47.1 %all-gather.16.cloned.1.call-done = bf16[2048,2048]{1,0:T(8,128)(2,1)} async-done(((bf16[2048,256]{1,0:T(8,128)(2,1)}), bf16[2048,2048]{1,0:T(8,128)(2,1)}) %all-gather.16.cloned.1.call-update) | async-done | bytes 8388624 | tf_op jit(solution)/shard_map/all_gather | solution.py:139
  411.7 15.3 %multiply_convert_fusion.1 = (bf16[512,2048]{1,0:T(8,128)(2,1)S(1)}, bf16[512,2048]{1,0:T(8,128)(2,1)}, bf16[512,2048]{1,0:T(8,128)(2,1)}) fusion(f32[512,2048]{1,0:T(8,128)} %fusion.87, f32[512,2048]{1,0:T(8,128)} %fusion.88, bf16[2048,2048]{1,0:T(8,128)(2,1)} %all-gather.16.cloned.1.call-done, f32[1,512,2048]{2,1,0:T(8,128)} %param.16), kind=kOutput, calls=%fused_computation.79 | convolution fusion | flops 4310695936 | bytes 27262976 | tf_op jit(solution)/shard_map/dot_general | solution.py:116
  427.0 8.4 fusion.89
  435.4 6.1 convolution_add_fusion
  441.6 9.8 convolution_convert_fusion
  451.7 145.0 %all-reduce.13.cloned.1.call-done = f32[512,2048]{1,0:T(8,128)} async-done(((f32[512,2048]{1,0:T(8,128)}), f32[512,2048]{1,0:T(8,128)}) %all-reduce.13.cloned.1.call-update) | async-done | bytes 4194320 | tf_op jit(solution)/shard_map/psum | solution.py:194
  596.7 4.5 multiply_reduce_fusion
  601.2 83.0 %all-reduce.11.cloned.1.call-done = bf16[512,2048]{1,0:T(8,128)(2,1)} async-done(((bf16[512,2048]{1,0:T(8,128)(2,1)}), bf16[512,2048]{1,0:T(8,128)(2,1)}) %all-reduce.11.cloned.1.call-update) | async-done | bytes 2097168 | tf_op jit(solution)/shard_map/psum | solution.py:189
  684.2 8.1 bitcast_add_fusion
  695.6 20.4 %while.27 = (s32[]{:T(128)}, f32[2,4,512,64]{2,3,1,0:T(8,128)}, f32[2,1024,64]{1,2,0:T(8,128)S(1)}, f32[2,1024,64]{1,2,0:T(8,128)}, pred[512,1024]{1,0:T(8,128)(...) while((s32[]{:T(128)}, f32[2,4,512,64]{2,3,1,0:T(8,128)}, ...), condition=%wide.region_12.13_spmd, body=%wide.region_10.12_spmd.sunk | while | flops 1365768192 | bytes 50255028 | solution.py:112
  697.1 3.3 multiply_convert_fusion.7
  702.8 3.1 fusion.170
  707.3 3.3 multiply_convert_fusion.7
  713.0 3.1 fusion.170
  726.8 3.5 fusion.92
  732.2 5.7 fusion.73
  738.0 3.3 fusion.69
  742.9 9.7 fusion.93
  752.7 9.9 fusion.94
  764.1 10.4 fusion.82
  776.4 105.3 %all-reduce.15.cloned.1.call-done = f32[512,2048]{1,0:T(8,128)} async-done(((f32[512,2048]{1,0:T(8,128)}), f32[512,2048]{1,0:T(8,128)}) %all-reduce.15.cloned.1.call-update) | async-done | bytes 4194320 | tf_op jit(solution)/shard_map/psum | solution.py:220
  881.7 4.5 fusion.61
  886.2 24.1 %all-reduce.3 = (f32[2048]{0:T(1024)S(1)}, f32[2048]{0:T(1024)S(1)}) all-reduce(f32[2048]{0:T(1024)S(1)} %get-tuple-element.169, f32[2048]{0:T(1024)S(1)} %get-tuple-element.167), channel_id=9, replica_groups=mesh['fsdp'=4,'ctx'=2,'tp'=4] {'fsdp','ctx'}, use_global_device_ids=true, to_apply=%region_23.24.clone | all-reduce | flops 4096 | bytes 32768
  911.6 7.8 fusion.58
  920.3 39.8 %reduce-scatter.10.cloned.1.call-done = f32[256,128]{1,0:T(8,128)} async-done(((f32[2048,128]{1,0:T(8,128)}), f32[256,128]{1,0:T(8,128)}) %reduce-scatter.10.cloned.1.call-update) | async-done | bytes 131088 | tf_op jit(solution)/shard_map/reduce_scatter | solution.py:225
  960.1 54.9 %reduce-scatter.14.cloned.1.call-done = f32[512,256]{1,0:T(8,128)} async-done(((f32[512,2048]{1,0:T(8,128)}), f32[512,256]{1,0:T(8,128)}) %reduce-scatter.14.cloned.1.call-update) | async-done | bytes 524304 | tf_op jit(solution)/shard_map/reduce_scatter | solution.py:227
  1015.0 55.1 %reduce-scatter.8.cloned.1.call-done = f32[256,512]{1,0:T(8,128)} async-done(((f32[2048,512]{1,0:T(8,128)}), f32[256,512]{1,0:T(8,128)}) %reduce-scatter.8.cloned.1.call-update) | async-done | bytes 524304 | tf_op jit(solution)/shard_map/reduce_scatter | solution.py:224
  1070.1 120.2 %reduce-scatter.16.cloned.1.call-done = f32[256,2048]{1,0:T(8,128)} async-done(((f32[2048,2048]{1,0:T(8,128)}), f32[256,2048]{1,0:T(8,128)}) %reduce-scatter.16.cloned.1.call-update) | async-done | bytes 2097168 | tf_op jit(solution)/shard_map/reduce_scatter | solution.py:228
  1190.3 120.2 %reduce-scatter.18.cloned.1.call-done = f32[256,2048]{1,0:T(8,128)} async-done(((f32[2048,2048]{1,0:T(8,128)}), f32[256,2048]{1,0:T(8,128)}) %reduce-scatter.18.cloned.1.call-update) | async-done | bytes 2097168 | tf_op jit(solution)/shard_map/reduce_scatter | solution.py:229
  1310.5 120.0 %reduce-scatter.20.cloned.1.call-done = f32[2048,256]{1,0:T(8,128)} async-done(((f32[2048,2048]{1,0:T(8,128)}), f32[2048,256]{1,0:T(8,128)}) %reduce-scatter.20.cloned.1.call-update) | async-done | bytes 2097168 | tf_op jit(solution)/shard_map/reduce_scatter | solution.py:230
  (173 shorter events, 61.7 us)
Async XLA Ops:
  7.2 52.1 %all-gather.8.cloned.1.call-start = ((), (), s32[]{:S(2)}) async-start(), calls=%async_computation.7 | async-start | bytes 2359296 | tf_op jit(solution)/shard_map/all_gather | solution.py:133
  7.9 75.1 %all-gather.10.cloned.1.call-start = ((), (), s32[]{:S(2)}) async-start(), calls=%async_computation.8 | async-start | bytes 2359296 | tf_op jit(solution)/shard_map/all_gather | solution.py:136
  19.0 29.3 %copy-start.20 = (f32[8,1,256]{2,1,0:T(1,128)}, f32[8,1,256]{2,1,0:T(1,128)S(1)}, u32[]{:S(2)}) copy-start(f32[8,1,256]{2,1,0:T(1,128)S(1)} %convert_element_type.149) | copy-start | bytes 24580
  29.7 4.8 copy-start.7
  29.9 4.6 copy-start
  33.5 14.8 %copy-start.23 = (f32[512]{0:T(512)}, f32[512]{0:T(512)S(1)}, u32[]{:S(2)}) copy-start(f32[512]{0:T(512)S(1)} %get-tuple-element.236) | copy-start | bytes 6148
  34.5 31.6 %copy-start.13 = (f32[512,32]{0,1:T(8,128)}, f32[512,32]{0,1:T(8,128)S(1)}, u32[]{:S(2)}) copy-start(f32[512,32]{0,1:T(8,128)S(1)} %get-tuple-element.234) | copy-start | bytes 196612
  34.5 4.9 copy-start.22
  34.9 28.2 %copy-start.2 = (bf16[1,512,2048]{2,1,0:T(8,128)(2,1)}, bf16[1,512,2048]{2,1,0:T(8,128)(2,1)S(1)}, u32[]{:S(2)}) copy-start(bf16[1,512,2048]{2,1,0:T(8,128)(2,1)S(1)} %multiply_convert_fusion.5) | copy-start | bytes 6291460
  36.5 18.2 %collective-permute-start = (bf16[512,128]{0,1:T(8,128)(2,1)}, bf16[512,128]{0,1:T(8,128)(2,1)}, u32[]{:S(2)}, u32[]{:S(2)}) collective-permute-start(bf16[512,128]{0,1:T(8,128)(2,1)} %bitcast.31), channel_id=1, source_target_pairs={{0,4},{1,5},{2,6},{3,7},{8,12},{9,13},{10,14},{11,15},{16,20},{17,... | collective-permute-start | bytes 393224 | tf_op jit(solution)/shard_map/ppermute | solution.py:15
  48.3 3.2 copy-start.9
  51.5 4.2 collective-permute-start.1
  54.5 188.6 %all-reduce.9.cloned.1.call-start = ((), (), s32[]{:S(2)}) async-start(), calls=%async_computation.9 | async-start | bytes 8388608 | tf_op jit(solution)/shard_map/psum | solution.py:181
  67.9 2.4 copy-start.18
  74.3 2.4 copy-start.18
  87.9 1.8 copy-start.27
  87.9 210.1 %all-gather.12.cloned.1.call-start = ((), (), s32[]{:S(2)}) async-start(), calls=%async_computation.10 | async-start | bytes 9437184 | tf_op jit(solution)/shard_map/all_gather | solution.py:137
  88.5 265.6 %all-gather.14.cloned.1.call-start = ((), (), s32[]{:S(2)}) async-start(), calls=%async_computation.11 | async-start | bytes 9437184 | tf_op jit(solution)/shard_map/all_gather | solution.py:138
  89.1 322.6 %all-gather.16.cloned.1.call-start = ((), (), s32[]{:S(2)}) async-start(), calls=%async_computation.12 | async-start | bytes 9437184 | tf_op jit(solution)/shard_map/all_gather | solution.py:139
  89.7 507.0 %all-reduce.13.cloned.1.call-start = ((), (), s32[]{:S(2)}) async-start(), calls=%async_computation.14 | async-start | bytes 8388608 | tf_op jit(solution)/shard_map/psum | solution.py:194
  247.0 2.0 copy-start.1
  426.9 8.4 copy-start.30
  426.9 8.4 copy-start.26
  441.6 242.6 %all-reduce.11.cloned.1.call-start = ((), (), s32[]{:S(2)}) async-start(), calls=%async_computation.13 | async-start | bytes 4194304 | tf_op jit(solution)/shard_map/psum | solution.py:189
  451.4 430.3 %all-reduce.15.cloned.1.call-start = ((), (), s32[]{:S(2)}) async-start(), calls=%async_computation.15 | async-start | bytes 8388608 | tf_op jit(solution)/shard_map/psum | solution.py:220
  684.2 10.1 copy-start.12
  692.3 2.0 copy-start.4
  692.3 3.3 copy-start.19
  695.6 24.5 %copy-start.14 = (f32[512,32]{0,1:T(8,128)S(1)}, f32[512,32]{0,1:T(8,128)}, u32[]{:S(2)}) copy-start(f32[512,32]{0,1:T(8,128)} %copy-done.13) | copy-start | bytes 196612
  695.6 24.5 %copy-start.17 = (f32[512,32]{0,1:T(8,128)S(1)}, f32[512,32]{0,1:T(8,128)}, u32[]{:S(2)}) copy-start(f32[512,32]{0,1:T(8,128)} %get-tuple-element.232) | copy-start | bytes 196612
  697.0 3.3 copy-start.15
  707.3 3.3 copy-start.15
  716.1 5.5 copy-start.6
  717.3 6.5 collective-permute-start.3
  718.6 4.3 collective-permute-start.2
  726.8 3.6 copy-start.3
  726.8 193.6 %reduce-scatter.12.cloned.1.call-start = ((), (), s32[]{:S(2)}) async-start(), calls=%async_computation.18 | async-start | bytes 1179648 | tf_op jit(solution)/shard_map/reduce_scatter | solution.py:226
  730.3 229.8 %reduce-scatter.10.cloned.1.call-start = ((), (), s32[]{:S(2)}) async-start(), calls=%async_computation.17 | async-start | bytes 1179648 | tf_op jit(solution)/shard_map/reduce_scatter | solution.py:225
  732.2 282.8 %reduce-scatter.14.cloned.1.call-start = ((), (), s32[]{:S(2)}) async-start(), calls=%async_computation.19 | async-start | bytes 4718592 | tf_op jit(solution)/shard_map/reduce_scatter | solution.py:227
  737.9 332.2 %reduce-scatter.8.cloned.1.call-start = ((), (), s32[]{:S(2)}) async-start(), calls=%async_computation.16 | async-start | bytes 4718592 | tf_op jit(solution)/shard_map/reduce_scatter | solution.py:224
  741.3 1.6 copy-start.11
  741.3 449.0 %reduce-scatter.16.cloned.1.call-start = ((), (), s32[]{:S(2)}) async-start(), calls=%async_computation.20 | async-start | bytes 18874368 | tf_op jit(solution)/shard_map/reduce_scatter | solution.py:228
  752.6 557.9 %reduce-scatter.18.cloned.1.call-start = ((), (), s32[]{:S(2)}) async-start(), calls=%async_computation.21 | async-start | bytes 18874368 | tf_op jit(solution)/shard_map/reduce_scatter | solution.py:229
  762.6 1.6 copy-start.29
  762.6 668.0 %reduce-scatter.20.cloned.1.call-start = ((), (), s32[]{:S(2)}) async-start(), calls=%async_computation.22 | async-start | bytes 18874368 | tf_op jit(solution)/shard_map/reduce_scatter | solution.py:230
  774.5 107.2 %copy-start.21 = (f32[8,1,256]{2,1,0:T(1,128)S(1)}, f32[8,1,256]{2,1,0:T(1,128)}, u32[]{:S(2)}) copy-start(f32[8,1,256]{2,1,0:T(1,128)} %copy-done.20) | copy-start | bytes 24580
  774.6 107.2 %copy-start.24 = (f32[512]{0:T(512)S(1)}, f32[512]{0:T(512)}, u32[]{:S(2)}) copy-start(f32[512]{0:T(512)} %copy-done.23) | copy-start | bytes 6148
  776.4 135.1 %copy-start.25 = (f32[512]{0:T(512)S(1)}, f32[512]{0:T(512)}, u32[]{:S(2)}) copy-start(f32[512]{0:T(512)} %get-tuple-element.235) | copy-start | bytes 6148
  (6 other events, 6.5 us)
Sparse Core Ops, SparseCore 0:
  9.9 31.1 all-gather.7
  54.6 28.3 all-gather.9
  88.0 154.9 all-reduce.8
  244.8 53.2 all-gather.11
  299.8 54.2 all-gather.13
  355.8 55.8 all-gather.15
  441.7 154.9 all-reduce.12
  599.0 85.0 all-reduce.10
  726.9 154.7 all-reduce.14
  885.3 34.9 reduce-scatter.11
  924.1 35.9 reduce-scatter.9
  963.9 51.0 reduce-scatter.13
  1018.9 51.1 reduce-scatter.7
  1074.1 116.1 reduce-scatter.15
  1194.3 116.1 reduce-scatter.17
  1314.5 115.9 reduce-scatter.19
where the time goes:
time: 1450 us; the launch traced here: 1440 us
  waiting for transfers between devices  1130 us (78%)
  matrix products  149 us (10%)
  blocking collectives  63.1 us (4%)
  other arithmetic  46.2 us (3%)
  local copies, waits for them, and re-layouts  19 us (1%)
  between operations  15.6 us (1%)
    psum x1, waiting for transfers between devices, body(): d_hnorm = lax.psum(dotf(d_gate, wg.T) + dotf(d_up, wu.T), 'tp')  145 us
    psum x1, waiting for transfers between devices, body(): hidden = rows + lax.psum(dotf(attn_flat, wo), 'tp')  144 us
    dot_general x21, matrix products, dotf(): return jnp.dot(left, right, preferred_element_type=jnp.float32)  121 us
    reduce_scatter x1, waiting for transfers between devices, body(): lax.psum_scatter(dotf(hnorm.T, d_gate), ('fsdp', 'ctx'), scatter_dimensio...  120 us
    reduce_scatter x1, waiting for transfers between devices, body(): lax.psum_scatter(dotf(hnorm.T, d_up), ('fsdp', 'ctx'), scatter_dimension=...  120 us
    reduce_scatter x1, waiting for transfers between devices, body(): lax.psum_scatter(dotf(inner.T, cot_b), ('fsdp', 'ctx'), scatter_dimension...  120 us
    psum x1, waiting for transfers between devices, body(): lax.psum(dotf(dq_b, wq.T) + dotf(dk_b, wk.T) + dotf(dv_b, wv.T), 'tp')  105 us
    psum x1, waiting for transfers between devices, body(): lax.psum(dotf(inner, wd).astype(jnp.bfloat16), 'tp').astype(jnp.float32)  83 us
  transfers between devices with their start and end apart: 20, of which 15 were waited for; matrix products, arithmetic and copies ran while one was open for 9% of the time, Pallas kernels for 0%

commit v1 on v0

--- a/solution.py
+++ b/solution.py
@@ -7,6 +7,31 @@
 EPS = 1e-05
 BASE = 500000.0
 NEG = -1e30
+
+
+def follow_view(sheet, dim_k):
+    newest = list(sheet.shape[1:])
+    newest[dim_k] *= sheet.shape[0]
+    return jnp.moveaxis(sheet, 0, dim_k).reshape(newest)
+
+
+def pass_column(u_in, lane_axis):
+    size_here = lax.axis_size(lane_axis)
+    reply = u_in[None]
+    for it in range(size_here.bit_length() - 1):
+        everything = 1 << it
+        in_order = []
+        for s in range(size_here):
+            in_order.append((s, s ^ everything))
+        arr_now = lax.ppermute(reply, lane_axis, in_order)
+        val = jnp.stack([reply, arr_now], 0)
+        parts_out = lax.axis_index(lane_axis) >> it & 1
+        reply = jnp.where(parts_out == 0, val, val[::-1]).reshape(-1, *u_in.shape)
+    return reply
+
+
+def choose_ways_all(tile_in, xx, along_dim):
+    return follow_view(pass_column(tile_in, xx), along_dim)
 
 
 def shifted(shard, axis, by):
@@ -135,7 +160,7 @@
         lax.all_gather(w_value, ("fsdp", "ctx"), axis=0, tiled=True),
         lax.all_gather(w_output, ("fsdp", "ctx"), axis=1, tiled=True),
         lax.all_gather(w_gate, ("fsdp", "ctx"), axis=0, tiled=True),
-        lax.all_gather(w_up, ("fsdp", "ctx"), axis=0, tiled=True),
+        choose_ways_all(w_up, ("fsdp", "ctx"), 0),
         lax.all_gather(w_down, ("fsdp", "ctx"), axis=1, tiled=True),
         lax.all_gather(attn_gain, ("fsdp", "ctx"), axis=0, tiled=True),
         lax.all_gather(ffn_gain, ("fsdp", "ctx"), axis=0, tiled=True),

time: 1450 us -> 1400 us (0.966)
  waiting for transfers between devices: 1130 us -> 969 us
  blocking collectives: 63.1 us -> 149 us
  other arithmetic: 46.2 us -> 78.1 us
    psum x1, waiting for transfers between devices: 144 us -> 0.01 us  [body(): hidden = rows + lax.psum(dotf(attn_flat, wo), 'tp')]
    all_gather x1, blocking collectives: 9.09 us -> 95 us  [body(): lax.all_gather(ffn_gain, ('fsdp', 'ctx'), axis=0, tiled=True)]
    ppermute x0 -> x3, waiting for transfers between devices: none -> 49.2 us  [pass_column(): arr_now = lax.ppermute(reply, lane_axis, in_order)]
    all_gather x1 -> x0, waiting for transfers between devices: 45.5 us -> none  [body(): lax.all_gather(w_up, ('fsdp', 'ctx'), axis=0, tiled=True)]
    all_gather x1, waiting for transfers between devices: 47.2 us -> 22 us  [body(): lax.all_gather(w_gate, ('fsdp', 'ctx'), axis=0, tiled=True)]
    select_n x0 -> x2, other arithmetic: none -> 17.4 us  [pass_column(): reply = jnp.where(parts_out == 0, val, val[::-1]).reshape(-1, *u_in.shape)]
    another operation x3 -> x7, other arithmetic: 0.17 us -> 14.7 us  [the longest x4 14.5 us: pass_column(): val = jnp.stack([reply, arr_now], 0)]
  transfers between devices with their start and end apart: 20 -> 22, of which waited for: 15 -> 15; matrix products, arithmetic and copies ran while one was open for 9% -> 11% of each run, Pallas kernels for 0% -> 0%
where the time goes in v1:
time: 1400 us; the launch traced here: 1390 us
  waiting for transfers between devices  969 us (69%)
  blocking collectives  149 us (11%)
  matrix products  143 us (10%)
  other arithmetic  78.1 us (6%)
  local copies, waits for them, and re-layouts  19 us (1%)
  between operations  15.6 us (1%)
    psum x1, waiting for transfers between devices, body(): d_hnorm = lax.psum(dotf(d_gate, wg.T) + dotf(d_up, wu.T), 'tp')  145 us
    reduce_scatter x1, waiting for transfers between devices, body(): lax.psum_scatter(dotf(hnorm.T, d_gate), ('fsdp', 'ctx'), scatter_dimensio...  120 us
    reduce_scatter x1, waiting for transfers between devices, body(): lax.psum_scatter(dotf(hnorm.T, d_up), ('fsdp', 'ctx'), scatter_dimension=...  120 us
    reduce_scatter x1, waiting for transfers between devices, body(): lax.psum_scatter(dotf(inner.T, cot_b), ('fsdp', 'ctx'), scatter_dimension...  120 us
    dot_general x21, matrix products, dotf(): return jnp.dot(left, right, preferred_element_type=jnp.float32)  115 us
    psum x1, waiting for transfers between devices, body(): lax.psum(dotf(dq_b, wq.T) + dotf(dk_b, wk.T) + dotf(dv_b, wv.T), 'tp')  105 us
    all_gather x1, blocking collectives, body(): lax.all_gather(ffn_gain, ('fsdp', 'ctx'), axis=0, tiled=True)  95 us
    psum x1, waiting for transfers between devices, body(): lax.psum(dotf(inner, wd).astype(jnp.bfloat16), 'tp').astype(jnp.float32)  83.5 us
  transfers between devices with their start and end apart: 22, of which 15 were waited for; matrix products, arithmetic and copies ran while one was open for 11% of the time, Pallas kernels for 0%

profile of v1, /device:TPU:0, one launch (start us, length us, event | category | flops | bytes accessed | tf_op | source)
XLA Modules:
  0.0 1387.2 jit_solution(13115168115154881236)
XLA Ops:
  8.6 10.4 all-gather
  19.0 10.7 all_gather.26
  30.0 3.0 fusion.52
  36.5 2.9 collective-permute-start
  39.4 8.9 all_gather.27
  59.2 3.9 copy.28
  66.3 12.7 while.10
  79.0 4.0 all-gather.9.cloned.1.call-done
  83.0 4.9 fusion.89
  97.8 46.7 %collective-permute-done.3 = bf16[2,256,2048]{2,1,0:T(8,128)(2,1)} collective-permute-done((bf16[2,256,2048]{2,1,0:T(8,128)(2,1)}, bf16[2,256,2048]{2,1,0:T(8,128)(2,1)}, u32[]{:S(2)}, u32[]{:S(2)}) %collective-permute-start.3) | collective-permute-done | bytes 2097184 | tf_op jit(solution)/shard_map/ppermute | solution.py:26
  147.2 3.2 reverse_select_fusion.1
  151.4 95.0 %all-gather.1 = bf16[8,1,256]{2,1,0:T(2,128)(2,1)S(1)} all-gather(bf16[1,1,256]{2,1,0:T(2,128)(2,1)S(1)} %reshape.307), channel_id=1, replica_groups=mesh['fsdp'=4,'ctx'=2,'tp'=4] {'fsdp','ctx'}, dimensions={0}, use_global_device_ids=true | all-gather | bytes 4608 | tf_op jit(solution)/shard_map/all_gather | solution.py:166
  246.4 7.7 pad_maximum_fusion
  254.1 14.2 %reverse_select_fusion = bf16[2,4,256,2048]{3,2,1,0:T(8,128)(2,1)} fusion(bf16[2,4,256,2048]{3,2,1,0:T(8,128)(2,1)} %pad_maximum_fusion, pred[]{:T(512)S(6)} %eq.9), kind=kLoop, calls=%fused_computation.58 | loop fusion | flops 4194304 | bytes 16777216 | tf_op jit(solution)/shard_map/jit(_where)/select_n | solution.py:29
  268.3 4.0 multiply_reduce_fusion.2
  276.1 22.0 %all-gather.11.cloned.1.call-done = bf16[2048,2048]{1,0:T(8,128)(2,1)} async-done(((bf16[256,2048]{1,0:T(8,128)(2,1)}), bf16[2048,2048]{1,0:T(8,128)(2,1)}) %all-gather.11.cloned.1.call-update) | async-done | bytes 8388624 | tf_op jit(solution)/shard_map/all_gather | solution.py:162
  298.1 10.5 fusion.90
  308.6 47.1 %all-gather.13.cloned.1.call-done = bf16[2048,2048]{1,0:T(8,128)(2,1)} async-done(((bf16[2048,256]{1,0:T(8,128)(2,1)}), bf16[2048,2048]{1,0:T(8,128)(2,1)}) %all-gather.13.cloned.1.call-update) | async-done | bytes 8388624 | tf_op jit(solution)/shard_map/all_gather | solution.py:164
  355.7 8.8 fusion.83
  364.5 11.3 multiply_convert_fusion.1
  375.9 8.5 fusion.91
  384.4 6.1 convolution_add_fusion
  390.6 9.8 convolution_convert_fusion
  400.7 145.0 %all-reduce.13.cloned.1.call-done = f32[512,2048]{1,0:T(8,128)} async-done(((f32[512,2048]{1,0:T(8,128)}), f32[512,2048]{1,0:T(8,128)}) %all-reduce.13.cloned.1.call-update) | async-done | bytes 4194320 | tf_op jit(solution)/shard_map/psum | solution.py:219
  545.7 4.5 multiply_reduce_fusion
  550.2 83.5 %all-reduce.11.cloned.1.call-done = bf16[512,2048]{1,0:T(8,128)(2,1)} async-done(((bf16[512,2048]{1,0:T(8,128)(2,1)}), bf16[512,2048]{1,0:T(8,128)(2,1)}) %all-reduce.11.cloned.1.call-update) | async-done | bytes 2097168 | tf_op jit(solution)/shard_map/psum | solution.py:214
  633.7 8.1 bitcast_add_fusion
  645.2 20.4 %while.27 = (s32[]{:T(128)}, f32[2,4,512,64]{2,3,1,0:T(8,128)}, f32[2,1024,64]{1,2,0:T(8,128)S(1)}, f32[2,1024,64]{1,2,0:T(8,128)}, pred[512,1024]{1,0:T(8,128)(...) while((s32[]{:T(128)}, f32[2,4,512,64]{2,3,1,0:T(8,128)}, ...), condition=%wide.region_12.13_spmd, body=%wide.region_10.12_spmd.sunk | while | flops 1365768192 | bytes 50255028 | solution.py:137
  646.6 3.3 multiply_convert_fusion.7
  652.3 3.1 fusion.172
  656.8 3.3 multiply_convert_fusion.7
  662.5 3.1 fusion.172
  676.3 3.5 fusion.94
  681.7 5.7 fusion.75
  687.5 3.3 fusion.69
  692.4 9.7 fusion.95
  702.2 9.9 fusion.96
  713.7 10.4 fusion.85
  726.0 105.3 %all-reduce.15.cloned.1.call-done = f32[512,2048]{1,0:T(8,128)} async-done(((f32[512,2048]{1,0:T(8,128)}), f32[512,2048]{1,0:T(8,128)}) %all-reduce.15.cloned.1.call-update) | async-done | bytes 4194320 | tf_op jit(solution)/shard_map/psum | solution.py:245
  831.3 4.5 fusion.61
  835.8 24.1 %all-reduce.3 = (f32[2048]{0:T(1024)S(1)}, f32[2048]{0:T(1024)S(1)}) all-reduce(f32[2048]{0:T(1024)S(1)} %get-tuple-element.169, f32[2048]{0:T(1024)S(1)} %get-tuple-element.167), channel_id=9, replica_groups=mesh['fsdp'=4,'ctx'=2,'tp'=4] {'fsdp','ctx'}, use_global_device_ids=true, to_apply=%region_23.24.clone | all-reduce | flops 4096 | bytes 32768
  861.1 7.8 fusion.58
  870.0 39.6 %reduce-scatter.10.cloned.1.call-done = f32[256,128]{1,0:T(8,128)} async-done(((f32[2048,128]{1,0:T(8,128)}), f32[256,128]{1,0:T(8,128)}) %reduce-scatter.10.cloned.1.call-update) | async-done | bytes 131088 | tf_op jit(solution)/shard_map/reduce_scatter | solution.py:250
  909.6 55.0 %reduce-scatter.14.cloned.1.call-done = f32[512,256]{1,0:T(8,128)} async-done(((f32[512,2048]{1,0:T(8,128)}), f32[512,256]{1,0:T(8,128)}) %reduce-scatter.14.cloned.1.call-update) | async-done | bytes 524304 | tf_op jit(solution)/shard_map/reduce_scatter | solution.py:252
  964.7 55.0 %reduce-scatter.8.cloned.1.call-done = f32[256,512]{1,0:T(8,128)} async-done(((f32[2048,512]{1,0:T(8,128)}), f32[256,512]{1,0:T(8,128)}) %reduce-scatter.8.cloned.1.call-update) | async-done | bytes 524304 | tf_op jit(solution)/shard_map/reduce_scatter | solution.py:249
  1019.6 120.4 %reduce-scatter.16.cloned.1.call-done = f32[256,2048]{1,0:T(8,128)} async-done(((f32[2048,2048]{1,0:T(8,128)}), f32[256,2048]{1,0:T(8,128)}) %reduce-scatter.16.cloned.1.call-update) | async-done | bytes 2097168 | tf_op jit(solution)/shard_map/reduce_scatter | solution.py:253
  1140.0 120.2 %reduce-scatter.18.cloned.1.call-done = f32[256,2048]{1,0:T(8,128)} async-done(((f32[2048,2048]{1,0:T(8,128)}), f32[256,2048]{1,0:T(8,128)}) %reduce-scatter.18.cloned.1.call-update) | async-done | bytes 2097168 | tf_op jit(solution)/shard_map/reduce_scatter | solution.py:254
  1260.2 120.0 %reduce-scatter.20.cloned.1.call-done = f32[2048,256]{1,0:T(8,128)} async-done(((f32[2048,2048]{1,0:T(8,128)}), f32[2048,256]{1,0:T(8,128)}) %reduce-scatter.20.cloned.1.call-update) | async-done | bytes 2097168 | tf_op jit(solution)/shard_map/reduce_scatter | solution.py:255
  (191 shorter events, 79.5 us)
Async XLA Ops:
  7.2 52.1 %all-gather.7.cloned.1.call-start = ((), (), s32[]{:S(2)}) async-start(), calls=%async_computation.7 | async-start | bytes 2359296 | tf_op jit(solution)/shard_map/all_gather | solution.py:158
  7.9 75.1 %all-gather.9.cloned.1.call-start = ((), (), s32[]{:S(2)}) async-start(), calls=%async_computation.8 | async-start | bytes 2359296 | tf_op jit(solution)/shard_map/all_gather | solution.py:161
  19.0 29.3 %copy-start.22 = (f32[8,1,256]{2,1,0:T(1,128)}, f32[8,1,256]{2,1,0:T(1,128)S(1)}, u32[]{:S(2)}) copy-start(f32[8,1,256]{2,1,0:T(1,128)S(1)} %convert_element_type.149) | copy-start | bytes 24580
  29.7 4.8 copy-start.7
  29.9 4.6 copy-start
  33.5 14.8 %copy-start.25 = (f32[512]{0:T(512)}, f32[512]{0:T(512)S(1)}, u32[]{:S(2)}) copy-start(f32[512]{0:T(512)S(1)} %get-tuple-element.238) | copy-start | bytes 6148
  34.5 31.6 %copy-start.14 = (f32[512,32]{0,1:T(8,128)}, f32[512,32]{0,1:T(8,128)S(1)}, u32[]{:S(2)}) copy-start(f32[512,32]{0,1:T(8,128)S(1)} %get-tuple-element.236) | copy-start | bytes 196612
  34.5 4.9 copy-start.24
  34.9 28.2 %copy-start.2 = (bf16[1,512,2048]{2,1,0:T(8,128)(2,1)}, bf16[1,512,2048]{2,1,0:T(8,128)(2,1)S(1)}, u32[]{:S(2)}) copy-start(bf16[1,512,2048]{2,1,0:T(8,128)(2,1)S(1)} %multiply_convert_fusion.5) | copy-start | bytes 6291460
  36.5 18.2 %collective-permute-start = (bf16[512,128]{0,1:T(8,128)(2,1)}, bf16[512,128]{0,1:T(8,128)(2,1)}, u32[]{:S(2)}, u32[]{:S(2)}) collective-permute-start(bf16[512,128]{0,1:T(8,128)(2,1)} %bitcast.31), channel_id=1, source_target_pairs={{0,4},{1,5},{2,6},{3,7},{8,12},{9,13},{10,14},{11,15},{16,20},{17,... | collective-permute-start | bytes 393224 | tf_op jit(solution)/shard_map/ppermute | solution.py:40
  48.4 3.2 copy-start.9
  51.5 4.2 collective-permute-start.1
  54.5 213.8 %all-reduce.9.cloned.1.call-start = ((), (), s32[]{:S(2)}) async-start(), calls=%async_computation.9 | async-start | bytes 8388608 | tf_op jit(solution)/shard_map/psum | solution.py:206
  74.3 2.4 copy-start.20
  87.9 210.1 %all-gather.11.cloned.1.call-start = ((), (), s32[]{:S(2)}) async-start(), calls=%async_computation.10 | async-start | bytes 9437184 | tf_op jit(solution)/shard_map/all_gather | solution.py:162
  88.5 267.2 %all-gather.13.cloned.1.call-start = ((), (), s32[]{:S(2)}) async-start(), calls=%async_computation.11 | async-start | bytes 9437184 | tf_op jit(solution)/shard_map/all_gather | solution.py:164
  89.1 456.6 %all-reduce.13.cloned.1.call-start = ((), (), s32[]{:S(2)}) async-start(), calls=%async_computation.13 | async-start | bytes 8388608 | tf_op jit(solution)/shard_map/psum | solution.py:219
  89.4 2.9 collective-permute-start.2
  96.5 48.1 %collective-permute-start.3 = (bf16[2,256,2048]{2,1,0:T(8,128)(2,1)}, bf16[2,256,2048]{2,1,0:T(8,128)(2,1)}, u32[]{:S(2)}, u32[]{:S(2)}) collective-permute-start(bf16[2,256,2048]{2,1,0:T(8,128)(2,1)} %get-tuple-element.221), channel_id=1, source_target_pairs={{0,8},{4,12},{8,0},{12,4},{16,24},{20,28},{24,16},{28,20},{1,9},{5... | collective-permute-start | bytes 6291464 | tf_op jit(solution)/shard_map/ppermute | solution.py:26
  147.1 4.3 copy-start.28
  150.3 96.1 %collective-permute-start.4 = (bf16[4,256,2048]{2,1,0:T(8,128)(2,1)}, bf16[4,256,2048]{2,1,0:T(8,128)(2,1)}, u32[]{:S(2)}, u32[]{:S(2)}) collective-permute-start(bf16[4,256,2048]{2,1,0:T(8,128)(2,1)} %bitcast.46), channel_id=1, source_target_pairs={{0,16},{4,20},{8,24},{12,28},{16,0},{20,4},{24,8},{28,12},{1,17},{... | collective-permute-start | bytes 12582920 | tf_op jit(solution)/shard_map/ppermute | solution.py:26
  355.7 8.8 copy-start.11
  355.7 28.7 %slice-start = ((s8[8388608]{0:T(1024)(128)(4,1)}), s8[4194304]{0:T(1024)(128)(4,1)S(1)}, s32[]{:S(2)}) async-start(s8[8388608]{0:T(1024)(128)(4,1)} %bitcast.257), calls=%async_computation.22 | async-start | bytes 8388608
  364.5 19.9 %slice-start.1 = ((s8[8388608]{0:T(1024)(128)(4,1)}), s8[4194304]{0:T(1024)(128)(4,1)S(1)}, s32[]{:S(2)}) async-start(s8[8388608]{0:T(1024)(128)(4,1)} %bitcast.257), calls=%async_computation.23 | async-start | bytes 8388608
  375.9 8.5 copy-start.32
  375.9 8.5 copy-start.31
  390.5 243.2 %all-reduce.11.cloned.1.call-start = ((), (), s32[]{:S(2)}) async-start(), calls=%async_computation.12 | async-start | bytes 4194304 | tf_op jit(solution)/shard_map/psum | solution.py:214
  400.4 430.8 %all-reduce.15.cloned.1.call-start = ((), (), s32[]{:S(2)}) async-start(), calls=%async_computation.14 | async-start | bytes 8388608 | tf_op jit(solution)/shard_map/psum | solution.py:245
  633.7 10.1 copy-start.13
  641.9 3.3 copy-start.21
  645.2 24.5 %copy-start.15 = (f32[512,32]{0,1:T(8,128)S(1)}, f32[512,32]{0,1:T(8,128)}, u32[]{:S(2)}) copy-start(f32[512,32]{0,1:T(8,128)} %copy-done.14) | copy-start | bytes 196612
  645.2 24.5 %copy-start.19 = (f32[512,32]{0,1:T(8,128)S(1)}, f32[512,32]{0,1:T(8,128)}, u32[]{:S(2)}) copy-start(f32[512,32]{0,1:T(8,128)} %get-tuple-element.234) | copy-start | bytes 196612
  646.6 3.3 copy-start.16
  656.8 3.3 copy-start.16
  665.6 5.5 copy-start.6
  666.8 6.5 collective-permute-start.6
  668.2 4.3 collective-permute-start.5
  676.3 3.6 copy-start.3
  676.3 193.7 %reduce-scatter.12.cloned.1.call-start = ((), (), s32[]{:S(2)}) async-start(), calls=%async_computation.17 | async-start | bytes 1179648 | tf_op jit(solution)/shard_map/reduce_scatter | solution.py:251
  679.8 229.8 %reduce-scatter.10.cloned.1.call-start = ((), (), s32[]{:S(2)}) async-start(), calls=%async_computation.16 | async-start | bytes 1179648 | tf_op jit(solution)/shard_map/reduce_scatter | solution.py:250
  681.7 283.0 %reduce-scatter.14.cloned.1.call-start = ((), (), s32[]{:S(2)}) async-start(), calls=%async_computation.18 | async-start | bytes 4718592 | tf_op jit(solution)/shard_map/reduce_scatter | solution.py:252
  687.4 332.2 %reduce-scatter.8.cloned.1.call-start = ((), (), s32[]{:S(2)}) async-start(), calls=%async_computation.15 | async-start | bytes 4718592 | tf_op jit(solution)/shard_map/reduce_scatter | solution.py:249
  690.8 449.2 %reduce-scatter.16.cloned.1.call-start = ((), (), s32[]{:S(2)}) async-start(), calls=%async_computation.19 | async-start | bytes 18874368 | tf_op jit(solution)/shard_map/reduce_scatter | solution.py:253
  702.2 558.1 %reduce-scatter.18.cloned.1.call-start = ((), (), s32[]{:S(2)}) async-start(), calls=%async_computation.20 | async-start | bytes 18874368 | tf_op jit(solution)/shard_map/reduce_scatter | solution.py:254
  712.1 668.1 %reduce-scatter.20.cloned.1.call-start = ((), (), s32[]{:S(2)}) async-start(), calls=%async_computation.21 | async-start | bytes 18874368 | tf_op jit(solution)/shard_map/reduce_scatter | solution.py:255
  724.1 107.2 %copy-start.23 = (f32[8,1,256]{2,1,0:T(1,128)S(1)}, f32[8,1,256]{2,1,0:T(1,128)}, u32[]{:S(2)}) copy-start(f32[8,1,256]{2,1,0:T(1,128)} %copy-done.22) | copy-start | bytes 24580
  724.1 107.2 %copy-start.26 = (f32[512]{0:T(512)S(1)}, f32[512]{0:T(512)}, u32[]{:S(2)}) copy-start(f32[512]{0:T(512)} %copy-done.25) | copy-start | bytes 6148
  726.0 135.1 %copy-start.27 = (f32[512]{0:T(512)S(1)}, f32[512]{0:T(512)}, u32[]{:S(2)}) copy-start(f32[512]{0:T(512)} %get-tuple-element.237) | copy-start | bytes 6148
  (12 other events, 17.5 us)
Sparse Core Ops, SparseCore 0:
  9.9 31.1 all-gather.6
  54.6 28.3 all-gather.8
  88.1 154.9 all-reduce.8
  244.8 53.2 all-gather.10
  299.8 55.8 all-gather.12
  390.7 154.9 all-reduce.12
  548.6 85.0 all-reduce.10
  676.4 154.8 all-reduce.14
  835.0 34.9 reduce-scatter.11
  873.6 35.9 reduce-scatter.9
  913.6 51.0 reduce-scatter.13
  968.4 51.1 reduce-scatter.7
  1023.8 116.1 reduce-scatter.15
  1144.0 116.1 reduce-scatter.17
  1264.2 115.9 reduce-scatter.19
